TPU v7x, 512 devices: a whole 4x4x16 slice. The times are simulated.
512 devices in a mesh: pages: 128 (over x, z, core), mp: 4 (over y).
Axes of the slice: x: 4, y: 4, z: 16, core: 2. Of those that a mesh axis runs over, the one named last changes fastest.
Arguments:
- queries: bfloat16 [256, 8192], P('pages', 'mp'), may hold values from -9 to 9
- cached_keys: bfloat16 [2048, 128, 8, 128], P('pages', None, 'mp'), may hold values from -8 to 8
- cached_values: bfloat16 [2048, 128, 8, 128], P('pages', None, 'mp'), may hold values from -4 to 4
- out_weight: bfloat16 [8192, 8192], P('mp', 'pages'), may hold values from -0.0625 to 0.0625
- select: int32 [2, 24], replicated, may hold values from 0 to 2047, as said below
- page_table: int32 [2048], replicated, may hold values from 0 to 2047, as said below
- block_page: int32 [2], replicated, may hold values from 0 to 2047, as said below
Outputs:
- mixed: bfloat16 [256, 8192], P('mp', 'pages')
Inputs may be any that keep to these rules, and one draw needn't show every extreme that they name: A permutation: each logical page has its own cache row, held by index page_table[p] // 16 of pages. `select`: each row holds 24 distinct pages: the block's own page block_page[b] and pages lying wholly before the block. They lie on exactly 4 owners, 6 on each. No owner holds selected pages of more than min(2, 4) blocks, and some owner holds that many. `block_page`: Distinct.
All inputs are finite; a program needn't handle non-finite values.
Results may differ from a plain program's by a relative error of at most 0.0063.
Values may be sent and summed in bfloat16 or wider, within the bound.
A program may use at most 64 MiB of HBM per device.

v0:
```python
import functools

import jax
import jax.numpy as jnp
from jax import lax
from jax.experimental import pallas as pl
from jax.experimental.pallas import tpu as pltpu
from jax.sharding import Mesh
from jax.sharding import PartitionSpec as P

PAGES = ("x", "z", "c")
MESH = pl.DeviceIdType.MESH
NX, NZ, NY = 4, 16, 4
PAGE = 128
PAGES_DEV = 16
PICKED = 6
BLOCKS = 2
HEADS = 8
HEAD = 128
SCALE = HEAD ** -0.5
FLOOR = -1e30
RIGHT = NZ // 2
LEFT = NZ // 2 - 1
VMEM = pltpu.MemorySpace.VMEM
DMA = pltpu.SemaphoreType.DMA


def around(value, size):
    return lax.rem(value + size, size)


def place():
    return tuple(lax.axis_index(axis) for axis in ("x", "z", "c", "y"))


def greet(peers):
    barrier = pltpu.get_barrier_semaphore()
    for peer in peers:
        pl.semaphore_signal(barrier, inc=1, device_id=peer, device_id_type=MESH)
    pl.semaphore_wait(barrier, len(peers))


def sent(source, target, send_sem, recv_sem, peer):
    copy = pltpu.make_async_remote_copy(
        src_ref=source,
        dst_ref=target,
        send_sem=send_sem,
        recv_sem=recv_sem,
        device_id=peer,
        device_id_type=MESH,
    )
    return copy


def spread(buffer, own, x, z, zs_r, zr_r, zs_l, zr_l, xs, xr):
    zr, zl = {"z": around(z + 1, NZ)}, {"z": around(z - 1, NZ)}
    started = []

    def along(slot, step, send, recv, peer):
        copy = sent(buffer.at[x, slot], buffer.at[x, slot], send.at[step], recv.at[step], peer)
        copy.start()
        started.append(copy)

    def across(slot, number):
        for j in range(1, NX):
            copy = sent(
                buffer.at[x, slot],
                buffer.at[x, slot],
                xs.at[j - 1, number],
                xr.at[j - 1, number],
                {"x": around(x + j, NX)},
            )
            copy.start()
            started.append(copy)

    def arrived(slot, sem):
        pltpu.make_async_copy(buffer.at[x, slot], buffer.at[x, slot], sem).wait()

    along(z, 0, zs_r, zr_r, zr)
    along(z, 0, zs_l, zr_l, zl)
    across(z, 0)
    for step in range(RIGHT):
        slot = around(z - 1 - step, NZ)
        arrived(slot, zr_r.at[step])
        if step + 1 < RIGHT:
            along(slot, step + 1, zs_r, zr_r, zr)
        across(slot, 1 + step)
        if step < LEFT:
            slot = around(z + 1 + step, NZ)
            arrived(slot, zr_l.at[step])
            if step + 1 < LEFT:
                along(slot, step + 1, zs_l, zr_l, zl)
            across(slot, 1 + RIGHT + step)
    for j in range(1, NX):
        far = around(x - j, NX)
        for number in range(NZ):
            if number == 0:
                slot = z
            elif number <= RIGHT:
                slot = around(z - number, NZ)
            else:
                slot = around(z + number - RIGHT, NZ)
            sem = xr.at[j - 1, number]
            pltpu.make_async_copy(buffer.at[far, slot], buffer.at[far, slot], sem).wait()
    return started


def collect_kernel(q, k, v, w, qall, kp, vp, wcat, ps, pr, ls, zs_r, zr_r, zs_l, zr_l, xs, xr):
    x, z, c, y = place()
    other = {"c": 1 - c}
    greet([other, {"z": around(z + 1, NZ)}, {"z": around(z - 1, NZ)}] + [{"x": around(x + j, NX)} for j in range(1, NX)])
    pair = [
        sent(q.at[1 - c], qall.at[x, z, c], ps.at[0], pr.at[0], other),
        sent(k, kp, ps.at[1], pr.at[1], other),
        sent(v, vp, ps.at[2], pr.at[2], other),
        sent(w.at[:, pl.ds((1 - c) * 1024, 1024)], wcat.at[c], ps.at[3], pr.at[3], other),
    ]
    mine = pltpu.make_async_copy(q.at[c], qall.at[x, z, c], ls.at[0])
    mine_w = pltpu.make_async_copy(w.at[:, pl.ds(c * 1024, 1024)], wcat.at[c], ls.at[1])
    pair[0].start()
    mine.start()
    for copy in pair[1:]:
        copy.start()
    mine_w.start()
    mine.wait()
    pltpu.make_async_copy(q.at[c], qall.at[x, z, 1 - c], pr.at[0]).wait()
    started = spread(qall, None, x, z, zs_r, zr_r, zs_l, zr_l, xs, xr)
    pltpu.make_async_copy(k, kp, pr.at[1]).wait()
    pltpu.make_async_copy(v, vp, pr.at[2]).wait()
    pltpu.make_async_copy(w.at[:, pl.ds(0, 1024)], wcat.at[1 - c], pr.at[3]).wait()
    mine_w.wait()
    for copy in pair + started:
        copy.wait_send()


SPREAD_SEMS = [DMA((RIGHT,)), DMA((RIGHT,)), DMA((LEFT,)), DMA((LEFT,)), DMA((NX - 1, NZ)), DMA((NX - 1, NZ))]


def collect(q, k, v, w):
    anywhere = pl.BlockSpec(memory_space=pl.ANY)
    inside = pl.BlockSpec(memory_space=VMEM)
    return pl.pallas_call(
        collect_kernel,
        out_shape=(
            jax.ShapeDtypeStruct((NX, NZ, 2, 16, HEAD), jnp.bfloat16),
            jax.ShapeDtypeStruct(k.shape, k.dtype),
            jax.ShapeDtypeStruct(v.shape, v.dtype),
            jax.ShapeDtypeStruct((2, 64, 1024), jnp.bfloat16),
        ),
        in_specs=[inside, anywhere, anywhere, anywhere],
        out_specs=(inside, anywhere, anywhere, anywhere),
        scratch_shapes=[DMA((4,)), DMA((4,)), DMA((2,))] + SPREAD_SEMS,
        compiler_params=pltpu.CompilerParams(collective_id=0, has_side_effects=True),
        name="collect",
    )(q, k, v, w)


def attend_kernel(
    select, table, block_page, q, ko, vo, kp, vp, out, stat,
    listed, counts, kraw, vraw, flat, keys, values, acc, tops, totals, ks, vs,
):
    x, z, c, y = place()
    chip = (x * NZ + z) * 2
    for block in range(BLOCKS):
        own_page = block_page[block]
        own_owner = lax.shift_right_logical(table[own_page], 4)
        for side in range(2):
            owner = chip + jnp.where(side == 0, c, 1 - c)
            first = jnp.where(own_owner == owner, 1, 0)

            def scan(i, n, block=block, side=side, owner=owner, own_page=own_page):
                page = select[block, i]
                row = table[page]
                hit = lax.shift_right_logical(row, 4) == owner
                at = jnp.where(page == own_page, 0, jnp.minimum(n, PICKED - 1))

                @pl.when(hit)
                def _():
                    listed[(block * 2 + side) * PICKED + at] = row & (PAGES_DEV - 1)

                return n + jnp.where(jnp.logical_and(hit, page != own_page), 1, 0)

            filled = lax.fori_loop(0, 4 * PICKED, scan, first)
            counts[block * 2 + side] = filled

            @pl.when(filled == PICKED)
            def _(block=block, side=side):
                combo = block * 2 + side
                for i in range(PICKED):
                    row = listed[combo * PICKED + i]
                    pltpu.make_async_copy((ko, kp)[side].at[row], kraw.at[combo, i], ks.at[combo, i]).start()
                    pltpu.make_async_copy((vo, vp)[side].at[row], vraw.at[combo, i], vs.at[combo, i]).start()

    spot = lax.broadcasted_iota(jnp.int32, (8, HEAD), 1)
    for block in range(BLOCKS):
        any_here = jnp.logical_or(counts[block * 2] == PICKED, counts[block * 2 + 1] == PICKED)
        lines = slice(block * 8, block * 8 + 8)

        @pl.when(jnp.logical_not(any_here))
        def _(lines=lines):
            out[:, lines] = jnp.zeros((NX, 8, 16, 256), jnp.bfloat16)
            stat[:, lines] = jnp.full((NX, 8, 8, HEAD), FLOOR, jnp.float32)

        @pl.when(any_here)
        def _(block=block, lines=lines):
            acc[...] = jnp.zeros(acc.shape, jnp.float32)
            tops[...] = jnp.full(tops.shape, FLOOR, jnp.float32)
            totals[...] = jnp.zeros(totals.shape, jnp.float32)
            for side in range(2):
                combo = block * 2 + side

                @pl.when(counts[combo] == PICKED)
                def _(side=side, combo=combo):
                    for i in range(PICKED):
                        pltpu.make_async_copy(ko.at[0], kraw.at[combo, i], ks.at[combo, i]).wait()
                        flat[...] = kraw[combo, i].astype(jnp.float32)
                        keys[pl.ds(i * PAGE, PAGE), :] = flat[pl.ds(c, PAGE, stride=2), :].astype(jnp.bfloat16)
                    for i in range(PICKED):
                        pltpu.make_async_copy(vo.at[0], vraw.at[combo, i], vs.at[combo, i]).wait()
                        flat[...] = vraw[combo, i].astype(jnp.float32)
                        values[pl.ds(i * PAGE, PAGE), :] = flat[pl.ds(c, PAGE, stride=2), :].astype(jnp.bfloat16)
                    own_owner = lax.shift_right_logical(table[block_page[block]], 4)
                    masked = own_owner == chip + jnp.where(side == 0, c, 1 - c)
                    slack = jnp.where(masked, 0, PAGE)

                    for part in range(4):
                        size = 256
                        rows = pl.ds(part * size, size)
                        qx = 2 * block + part // 2
                        queries = q[qx, (part % 2) * 8:(part % 2) * 8 + 8].reshape(size, HEAD)
                        scores = lax.dot_general(
                            queries, keys[...], (((1,), (1,)), ((), ())), preferred_element_type=jnp.float32
                        ) * SCALE
                        row = lax.broadcasted_iota(jnp.int32, (size, PAGE), 0) // HEADS + part * (size // HEADS)
                        key = lax.broadcasted_iota(jnp.int32, (size, PAGE), 1)
                        head = jnp.where(key <= row + slack, scores[:, :PAGE], FLOOR)
                        scores = jnp.concatenate([head, scores[:, PAGE:]], axis=1)
                        peak = jnp.max(scores, axis=1, keepdims=True)
                        weights = jnp.exp(scores - peak)
                        total = jnp.sum(weights, axis=1, keepdims=True)
                        got = jnp.dot(weights.astype(jnp.bfloat16), values[...], preferred_element_type=jnp.float32)
                        old = tops[rows, :]
                        new = jnp.maximum(old, peak)
                        keep = jnp.exp(old - new)
                        fresh = jnp.exp(peak - new)
                        tops[rows, :] = new
                        totals[rows, :] = totals[rows, :] * keep + total * fresh
                        acc[rows, :] = acc[rows, :] * keep + got * fresh

            acc[...] = acc[...] / totals[...]
            tops[...] = tops[...] + jnp.log(totals[...])
            for xd in range(NX):
                pieces = []
                for half in range(2):
                    head = 2 * xd + half
                    got = acc[pl.ds(head, PAGE, stride=HEADS), :].astype(jnp.bfloat16)
                    out[xd, lines, :, half * HEAD:(half + 1) * HEAD] = got.reshape(8, 16, HEAD)
                    top = tops[pl.ds(head, PAGE, stride=HEADS), :].reshape(8, 16, HEAD)
                    pieces.append(top)
                lane = spot[None]
                low = jnp.where(lane < 32, pieces[0][:, :8], pieces[1][:, :8])
                high = jnp.where(lane < 96, pieces[0][:, 8:], pieces[1][:, 8:])
                stat[xd, lines] = jnp.where(lane < 64, low, high)


def attend(select, table, block_page, q, ko, vo, kp, vp):
    anywhere = pl.BlockSpec(memory_space=pl.ANY)
    inside = pl.BlockSpec(memory_space=VMEM)
    scalars = pl.BlockSpec(memory_space=pltpu.MemorySpace.SMEM)
    combos = BLOCKS * 2
    return pl.pallas_call(
        attend_kernel,
        out_shape=(
            jax.ShapeDtypeStruct((NX, NZ, 16, 256), jnp.bfloat16),
            jax.ShapeDtypeStruct((NX, NZ, 8, HEAD), jnp.float32),
        ),
        in_specs=[scalars] * 3 + [inside] + [anywhere] * 4,
        out_specs=(inside, inside),
        scratch_shapes=[
            pltpu.SMEM((combos * PICKED,), jnp.int32),
            pltpu.SMEM((combos,), jnp.int32),
            pltpu.VMEM((combos, PICKED, 2 * PAGE, HEAD), jnp.bfloat16),
            pltpu.VMEM((combos, PICKED, 2 * PAGE, HEAD), jnp.bfloat16),
            pltpu.VMEM((2 * PAGE, HEAD), jnp.float32),
            pltpu.VMEM((PICKED * PAGE, HEAD), jnp.bfloat16),
            pltpu.VMEM((PICKED * PAGE, HEAD), jnp.bfloat16),
            pltpu.VMEM((PAGE * HEADS, HEAD), jnp.float32),
            pltpu.VMEM((PAGE * HEADS, HEAD), jnp.float32),
            pltpu.VMEM((PAGE * HEADS, HEAD), jnp.float32),
            DMA((combos, PICKED)),
            DMA((combos, PICKED)),
        ],
        name="attend",
    )(select, table, block_page, q, ko, vo, kp, vp)


def blended(items):
    top = items[0][1]
    for _, level in items[1:]:
        top = jnp.maximum(top, level)
    shares = [jnp.exp(level - top) for _, level in items]
    total = shares[0]
    for share in shares[1:]:
        total = total + share
    scale = 1.0 / total
    lines = [[None, None], [None, None]]
    for (value, _), share in zip(items, shares):
        share = share * scale
        for band in range(2):
            for half in range(2):
                lane = band * 64 + half * 32
                term = value[band * 8:(band + 1) * 8, half * HEAD:(half + 1) * HEAD] * share[:, lane:lane + 1]
                before = lines[band][half]
                lines[band][half] = term if before is None else before + term
    value = jnp.concatenate([jnp.concatenate(line, axis=1) for line in lines], axis=0)
    return value, top + jnp.log(total)


def merge_kernel(
    part, stat, w, result, got, got_stat, send_r, send_l, stat_r, stat_l, land_r, land_l, lstat_r, lstat_l,
    chunk, merged, terms, terms_in, sums, sums_in,
    gs, gr, hs, hr, rs, rr, rts, rtr, ls, lr, lts, ltr, cs, ys, yr, ps, pr,
    zs_r, zr_r, zs_l, zr_l, xs, xr,
):
    x, z, c, y = place()
    right, left = {"z": around(z + 1, NZ)}, {"z": around(z - 1, NZ)}
    other = {"c": 1 - c}
    xpeers = [{"x": around(x + j, NX)} for j in range(1, NX)]
    ypeers = [{"y": around(y + j, NY)} for j in range(1, NY)]
    greet([right, left, other] + xpeers + ypeers)
    started = []

    def go(copy):
        copy.start()
        started.append(copy)

    for j in range(1, NX):
        xd = around(x + j, NX)
        go(sent(stat.at[xd], got_stat.at[j - 1], hs.at[j - 1], hr.at[j - 1], xpeers[j - 1]))
    order = []
    for step in range(RIGHT):
        order.append(around(z + RIGHT - step, NZ))
        if step < LEFT:
            order.append(around(z - LEFT + step, NZ))
    order.append(z)
    for number, slot in enumerate(order):
        for j in range(1, NX):
            xd = around(x + j, NX)
            go(sent(part.at[xd, slot], got.at[j - 1, slot], gs.at[j - 1, number], gr.at[j - 1, number], xpeers[j - 1]))
    for j in range(NX - 1):
        pltpu.make_async_copy(got_stat.at[j], got_stat.at[j], hr.at[j]).wait()

    def crossed(number):
        slot = order[number]
        items = [(part[x, slot].astype(jnp.float32), stat[x, slot])]
        for j in range(NX - 1):
            pltpu.make_async_copy(got.at[j, slot], got.at[j, slot], gr.at[j, number]).wait()
            items.append((got[j, slot].astype(jnp.float32), got_stat[j, slot]))
        return blended(items)

    def hop(step, value, send, send_stat, land, land_stat, sems, peer):
        if step > 0:
            pltpu.make_async_copy(land.at[step - 1], land.at[step - 1], sems[1].at[step - 1]).wait()
            pltpu.make_async_copy(land_stat.at[step - 1], land_stat.at[step - 1], sems[3].at[step - 1]).wait()
            value = blended([value, (land[step - 1].astype(jnp.float32), land_stat[step - 1])])
        send[step] = value[0].astype(jnp.bfloat16)
        send_stat[step] = value[1]
        go(sent(send.at[step], land.at[step], sems[0].at[step], sems[1].at[step], peer))
        go(sent(send_stat.at[step], land_stat.at[step], sems[2].at[step], sems[3].at[step], peer))

    number = 0
    for step in range(RIGHT):
        value = crossed(number)
        number += 1
        if step < LEFT:
            second = crossed(number)
            number += 1
        hop(step, value, send_r, stat_r, land_r, lstat_r, (rs, rr, rts, rtr), right)
        if step < LEFT:
            hop(step, second, send_l, stat_l, land_l, lstat_l, (ls, lr, lts, ltr), left)
    items = [crossed(number)]
    for land, land_stat, sem, sem_stat, last in (
        (land_r, lstat_r, rr, rtr, RIGHT - 1),
        (land_l, lstat_l, lr, ltr, LEFT - 1),
    ):
        pltpu.make_async_copy(land.at[last], land.at[last], sem.at[last]).wait()
        pltpu.make_async_copy(land_stat.at[last], land_stat.at[last], sem_stat.at[last]).wait()
        items.append((land[last].astype(jnp.float32), land_stat[last]))
    chunk[...] = blended(items)[0].astype(jnp.bfloat16)
    mine = pltpu.make_async_copy(chunk, merged.at[x, z], cs)
    mine.start()
    mine.wait()
    started.extend(spread(merged, None, x, z, zs_r, zr_r, zs_l, zr_l, xs, xr))
    weight = w[...].reshape(128, 1024)
    total = None
    for xd in range(NX):
        term = lax.dot_general(
            merged[xd].reshape(256, 256),
            weight[:, xd * 256:(xd + 1) * 256],
            (((1,), (1,)), ((), ())),
            preferred_element_type=jnp.float32,
        )
        total = term if total is None else total + term
    terms[...] = total.reshape(NY, 64, 128)
    for j in range(1, NY):
        go(sent(terms.at[around(y + j, NY)], terms_in.at[j - 1], ys.at[j - 1], yr.at[j - 1], ypeers[j - 1]))
    total = terms[y]
    for j in range(NY - 1):
        pltpu.make_async_copy(terms_in.at[j], terms_in.at[j], yr.at[j]).wait()
        total = total + terms_in[j]
    sums[...] = total
    go(sent(sums, sums_in, ps, pr, other))
    pltpu.make_async_copy(sums_in, sums_in, pr).wait()
    total = sums[...] + sums_in[...]
    result[...] = jnp.where(c == 0, total[:, :64], total[:, 64:]).astype(jnp.bfloat16)
    for copy in started:
        copy.wait_send()


def merge(part, stat, w):
    inside = pl.BlockSpec(memory_space=VMEM)
    small = lambda n: pltpu.VMEM((n, 16, 256), jnp.bfloat16)
    level = lambda n: pltpu.VMEM((n, 8, HEAD), jnp.float32)
    return pl.pallas_call(
        merge_kernel,
        out_shape=jax.ShapeDtypeStruct((64, 64), jnp.bfloat16),
        in_specs=[inside] * 3,
        out_specs=inside,
        scratch_shapes=[
            pltpu.VMEM((NX - 1, NZ, 16, 256), jnp.bfloat16),
            pltpu.VMEM((NX - 1, NZ, 8, HEAD), jnp.float32),
            small(RIGHT), small(LEFT), level(RIGHT), level(LEFT),
            small(RIGHT), small(LEFT), level(RIGHT), level(LEFT),
            pltpu.VMEM((16, 256), jnp.bfloat16),
            pltpu.VMEM((NX, NZ, 16, 256), jnp.bfloat16),
            pltpu.VMEM((NY, 64, 128), jnp.float32),
            pltpu.VMEM((NY - 1, 64, 128), jnp.float32),
            pltpu.VMEM((64, 128), jnp.float32),
            pltpu.VMEM((64, 128), jnp.float32),
            DMA((NX - 1, NZ)), DMA((NX - 1, NZ)), DMA((NX - 1,)), DMA((NX - 1,)),
            DMA((RIGHT,)), DMA((RIGHT,)), DMA((RIGHT,)), DMA((RIGHT,)),
            DMA((LEFT,)), DMA((LEFT,)), DMA((LEFT,)), DMA((LEFT,)),
            DMA, DMA((NY - 1,)), DMA((NY - 1,)), DMA, DMA,
        ] + SPREAD_SEMS,
        compiler_params=pltpu.CompilerParams(collective_id=1, has_side_effects=True),
        name="merge",
    )(part, stat, w)


def per_device(queries, cached_keys, cached_values, out_weight, select, page_table, block_page):
    q = queries.reshape(2, 2, HEADS, HEAD).transpose(1, 0, 2, 3).reshape(2, 16, HEAD)
    k = cached_keys.reshape(PAGES_DEV, 2 * PAGE, HEAD)
    v = cached_values.reshape(PAGES_DEV, 2 * PAGE, HEAD)
    qall, kp, vp, wcat = collect(q, k, v, out_weight.T)
    part, stat = attend(select, page_table, block_page, qall, k, v, kp, vp)
    return merge(part, stat, wcat)


def solution(mesh):
    torus = Mesh(mesh.devices.reshape(NX, NZ, 2, NY), ("x", "z", "c", "y"))
    return jax.shard_map(
        per_device,
        mesh=torus,
        in_specs=(
            P(PAGES, "y"),
            P(PAGES, None, "y", None),
            P(PAGES, None, "y", None),
            P("y", PAGES),
            P(),
            P(),
            P(),
        ),
        out_specs=P("y", PAGES),
        check_vma=False,
    )
```

profile of v0, /device:TPU:1, one launch (start us, length us, event | category | flops | bytes accessed | tf_op | source)
XLA Modules:
  0.0 119.8 jit_solution(7111441353067139727)
XLA Ops:
  0.0 1.3 %copy_bitcast_fusion.1.q = bf16[2,16,128]{2,1,0:T(8,128)(2,1)} fusion(bf16[1,2,16,128]{3,1,2,0:T(2,128)(2,1)} %bitcast.17), kind=kLoop, calls=%fused_computation.1 | loop fusion | bytes 16384 | tf_op jit(solution)/shard_map/reshape | solution.py:451
  1.3 36.5 %collect.1 = (bf16[4,16,2,16,128]{4,3,2,1,0:T(8,128)(2,1)}, bf16[16,256,128]{2,1,0:T(8,128)(2,1)}, bf16[16,256,128]{2,1,0:T(8,128)(2,1)}, bf16[2,64,1024]{2,1,0:T(8,128)(2,1)}) custom-call(bf16[2,16,128]{2,1,0:T(8,128)(2,1)} %copy_bitcast_fusion.1.q, bf16[16,256,128]{2,1,0:T(8,128)(2,1)} %bitcast.12, bf16[16,256,128]{2,1,0:T(8,128)(2,1)} %bitcast.14, ...), custom_call_target="tpu_custom_call" | custom-call | tf_op jit(solution)/shard_map/collect/pallas_call | solution.py:142
  37.8 4.1 %attend.1 = (bf16[4,16,16,256]{3,2,1,0:T(8,128)(2,1)}, f32[4,16,8,128]{3,2,1,0:T(8,128)}) custom-call(s32[2,24]{1,0:T(2,128)} %select.1, s32[2048]{0:T(1024)} %table.1, s32[2]{0:T(128)} %block_page.1, bf16[4,16,2,16,128]{4,3,2,1,0:T(8,128)(2,1)} %get-tuple-element.11.q, bf16[16,256,128]{2,1,0:T(8,128)(2,1)} %bitcast.13, bf16[16,256,128]{2,1,0:T(8,128)(2,1)} %bitcast.15, ...), custom_call_target="tpu_custom_call" | custom-call | tf_op jit(solution)/shard_map/attend/pallas_call | solution.py:271
  41.9 76.6 %merge.1 = bf16[64,64]{1,0:T(8,128)(2,1)} custom-call(bf16[4,16,16,256]{3,2,1,0:T(8,128)(2,1)} %get-tuple-element.14.part, f32[4,16,8,128]{3,2,1,0:T(8,128)} %get-tuple-element.15.stat, bf16[2,64,1024]{2,1,0:T(8,128)(2,1)} %get-tuple-element.16.w), custom_call_target="tpu_custom_call" | custom-call | tf_op jit(solution)/shard_map/merge/pallas_call | solution.py:424
  118.5 1.3 %copy.14 = bf16[64,64]{1,0:T(8,128)(2,1)} copy(bf16[64,64]{1,0:T(8,128)(2,1)} %merge.1) | data formatting | bytes 16384
where the time goes:
time: 120 us
  Pallas kernels  117 us (98%)
  local copies, waits for them, and re-layouts  2.62 us (2%)
    pallas_call x1, Pallas kernels, merge(): pl.pallas_call(merge_kernel, out_shape=jax.ShapeDtypeStruct((64, 64), jnp...  76.6 us
    pallas_call x1, Pallas kernels, collect(): pl.pallas_call(collect_kernel, out_shape=(jax.ShapeDtypeStruct((NX, NZ, 2...  36.5 us
    pallas_call x1, Pallas kernels, attend(): pl.pallas_call(attend_kernel, out_shape=(jax.ShapeDtypeStruct((NX, NZ, 16...  4.06 us

commit v1 on v0

v1 whole, which is shorter than its diff:
```python
import functools

import jax
import jax.numpy as jnp
from jax import lax
from jax.experimental import pallas as pl
from jax.experimental.pallas import tpu as pltpu
from jax.sharding import Mesh
from jax.sharding import PartitionSpec as P

PAGES = ("x", "z", "c")
MESH = pl.DeviceIdType.MESH
NX, NZ, NY = 4, 16, 4
PAGE = 128
PAGES_DEV = 16
PICKED = 6
BLOCKS = 2
HEADS = 8
HEAD = 128
SCALE = HEAD ** -0.5
FLOOR = -1e30
VMEM = pltpu.MemorySpace.VMEM
DMA = pltpu.SemaphoreType.DMA


def around(value, size):
    return lax.rem(value + size, size)


def place():
    return tuple(lax.axis_index(axis) for axis in ("x", "z", "c", "y"))


def greet(peers):
    barrier = pltpu.get_barrier_semaphore()
    for peer in peers:
        pl.semaphore_signal(barrier, inc=1, device_id=peer, device_id_type=MESH)
    pl.semaphore_wait(barrier, len(peers))


def sent(source, target, send_sem, recv_sem, peer):
    copy = pltpu.make_async_remote_copy(
        src_ref=source,
        dst_ref=target,
        send_sem=send_sem,
        recv_sem=recv_sem,
        device_id=peer,
        device_id_type=MESH,
    )
    return copy


def nearest(reverse=False):
    found = [hop for step in range(1, NZ // 2) for hop in (step, NZ - step)] + [NZ // 2]
    return found[::-1] if reverse else found


def arrived(target, sem):
    pltpu.make_async_copy(target, target, sem).wait()


def across(buffer, slot, number, xs, xr, x, started):
    for j in range(1, NX):
        copy = sent(
            buffer.at[x, slot], buffer.at[x, slot], xs.at[j - 1, number], xr.at[j - 1, number], {"x": around(x + j, NX)}
        )
        copy.start()
        started.append(copy)


def crossed(buffer, slot, number, xr, x):
    for j in range(1, NX):
        arrived(buffer.at[around(x - j, NX), slot], xr.at[j - 1, number])


def collect_kernel(
    select, table, block_page, q, k, v, w, lists, qall, kp, vp, wp, ps, pr, ls, zs, zr, xs, xr
):
    x, z, c, y = place()
    other = {"c": 1 - c}
    peers = [other] + [{"x": around(x + j, NX)} for j in range(1, NX)]
    for hop in nearest(True):
        for core in range(2):
            peers.append({"z": around(z + hop, NZ), "c": core})
    greet(peers)
    started = []

    def go(copy):
        copy.start()
        started.append(copy)

    for hop in nearest(True):
        for core in range(2):
            peer = {"z": around(z + hop, NZ), "c": core}
            go(sent(q.at[core], qall.at[x, z, c], zs.at[hop, core], zr.at[hop, c], peer))
    go(sent(q.at[1 - c], qall.at[x, z, c], zs.at[0, 0], zr.at[0, c], other))
    mine = pltpu.make_async_copy(q.at[c], qall.at[x, z, c], ls)
    mine.start()
    go(sent(k, kp, ps.at[0], pr.at[0], other))
    go(sent(v, vp, ps.at[1], pr.at[1], other))
    go(sent(w.at[:, pl.ds((1 - c) * 1024, 1024)], wp, ps.at[2], pr.at[2], other))
    mine.wait()
    arrived(qall.at[x, z, 1 - c], zr.at[0, 1 - c])
    across(qall, z, 0, xs, xr, x, started)
    chip = x * NZ + z
    for block in range(BLOCKS):
        own_page = block_page[block]
        own_row = table[own_page]
        own_chip = lax.shift_right_logical(own_row, 5)
        for side in range(2):
            core = c if side == 0 else 1 - c
            owner = chip * 2 + core
            has_own = (lax.shift_right_logical(own_row, 4) == owner).astype(jnp.int32)
            count = has_own
            spots = [jnp.where(has_own == 1, own_row & (PAGES_DEV - 1), 0)] + [0] * (PICKED - 1)

            def scan(i, carry, block=block, owner=owner, own_page=own_page):
                count, *spots = carry
                page = select[block, i]
                row = table[page]
                hit = jnp.logical_and(lax.shift_right_logical(row, 4) == owner, page != own_page)
                spots = [
                    jnp.where(jnp.logical_and(hit, count == n), row & (PAGES_DEV - 1), spot)
                    for n, spot in enumerate(spots)
                ]
                return (count + hit.astype(jnp.int32), *spots)

            spots = [jnp.int32(0) + spot for spot in spots]
            count, *spots = lax.fori_loop(0, 4 * PICKED, scan, (count, *spots))
            base = (block * 2 + side) * 8
            for n, spot in enumerate(spots):
                lists[base + n] = spot
            lists[base + PICKED] = count
            lists[base + PICKED + 1] = has_own
    for number, hop in enumerate(nearest()):
        slot = around(z - hop, NZ)
        arrived(qall.at[x, slot, 0], zr.at[hop, 0])
        arrived(qall.at[x, slot, 1], zr.at[hop, 1])
        across(qall, slot, 1 + number, xs, xr, x, started)
    for number, hop in enumerate([0] + nearest()):
        crossed(qall, around(z - hop, NZ), number, xr, x)
    arrived(kp, pr.at[0])
    arrived(vp, pr.at[1])
    arrived(wp, pr.at[2])
    for copy in started:
        copy.wait_send()


X_SEMS = [DMA((NX - 1, NZ)), DMA((NX - 1, NZ))]


def collect(select, table, block_page, q, k, v, w):
    anywhere = pl.BlockSpec(memory_space=pl.ANY)
    inside = pl.BlockSpec(memory_space=VMEM)
    scalars = pl.BlockSpec(memory_space=pltpu.MemorySpace.SMEM)
    return pl.pallas_call(
        collect_kernel,
        out_shape=(
            jax.ShapeDtypeStruct((BLOCKS * 2 * 8,), jnp.int32),
            jax.ShapeDtypeStruct((NX, NZ, 2, 16, HEAD), jnp.bfloat16),
            jax.ShapeDtypeStruct(k.shape, k.dtype),
            jax.ShapeDtypeStruct(v.shape, v.dtype),
            jax.ShapeDtypeStruct((64, 1024), jnp.bfloat16),
        ),
        in_specs=[scalars] * 3 + [inside, anywhere, anywhere, anywhere],
        out_specs=(scalars, inside, anywhere, anywhere, anywhere),
        scratch_shapes=[DMA((3,)), DMA((3,)), DMA, DMA((NZ, 2)), DMA((NZ, 2))] + X_SEMS,
        compiler_params=pltpu.CompilerParams(collective_id=0, has_side_effects=True),
        name="collect",
    )(select, table, block_page, q, k, v, w)


def attend_kernel(lists, q, ko, vo, kp, vp, out, stat, kraw, vraw, flat, keys, values, acc, tops, ks, vs):
    x, z, c, y = place()
    for combo in range(BLOCKS * 2):

        @pl.when(lists[combo * 8 + PICKED] == PICKED)
        def _(combo=combo):
            for i in range(PICKED):
                row = lists[combo * 8 + i]
                pltpu.make_async_copy((ko, kp)[combo % 2].at[row], kraw.at[combo, i], ks.at[combo, i]).start()
            for i in range(PICKED):
                row = lists[combo * 8 + i]
                pltpu.make_async_copy((vo, vp)[combo % 2].at[row], vraw.at[combo, i], vs.at[combo, i]).start()

    def unit(block, side, join):
        combo = block * 2 + side
        for i in range(PICKED):
            pltpu.make_async_copy(ko.at[0], kraw.at[combo, i], ks.at[combo, i]).wait()
            flat[i] = kraw[combo, i].astype(jnp.float32)
            keys[pl.ds(i * PAGE, PAGE), :] = flat[i, pl.ds(c, PAGE, stride=2), :].astype(jnp.bfloat16)
        for i in range(PICKED):
            pltpu.make_async_copy(vo.at[0], vraw.at[combo, i], vs.at[combo, i]).wait()
            flat[i] = vraw[combo, i].astype(jnp.float32)
            values[pl.ds(i * PAGE, PAGE), :] = flat[i, pl.ds(c, PAGE, stride=2), :].astype(jnp.bfloat16)
        slack = jnp.where(lists[combo * 8 + PICKED + 1] == 1, 0, PAGE)
        size = 256
        for part in range(PAGE * HEADS // size):
            rows = pl.ds(part * size, size)
            qx, qz = 2 * block + part // 2, part % 2 * 8
            queries = q[qx, qz:qz + 8].reshape(size, HEAD)
            scores = lax.dot_general(
                queries, keys[...], (((1,), (1,)), ((), ())), preferred_element_type=jnp.float32
            )
            line = lax.broadcasted_iota(jnp.int32, (size, PAGE), 0) + part * size
            row = lax.shift_left(lax.shift_right_logical(line, 4), 1) + (line & 1)
            key = lax.broadcasted_iota(jnp.int32, (size, PAGE), 1)
            head = jnp.where(key <= row + slack, scores[:, :PAGE], FLOOR)
            scores = jnp.concatenate([head, scores[:, PAGE:]], axis=1)
            peak = jnp.max(scores, axis=1, keepdims=True)
            weights = jnp.exp((scores - peak) * SCALE)
            total = jnp.sum(weights, axis=1, keepdims=True)
            got = jnp.dot(weights.astype(jnp.bfloat16), values[...], preferred_element_type=jnp.float32)
            got = got / total
            top = jnp.broadcast_to(peak * SCALE + jnp.log(total), (size, HEAD))
            if join:
                old = tops[rows, :]
                new = jnp.maximum(old, top)
                keep = jnp.exp(old - new)
                fresh = jnp.exp(top - new)
                total = keep + fresh
                got = (acc[rows, :] * keep + got * fresh) / total
                top = new + jnp.log(total)
            tops[rows, :] = top
            acc[rows, :] = got

    lane = lax.broadcasted_iota(jnp.int32, (4, 8, HEAD), 2)
    for block in range(BLOCKS):
        near = lists[block * 16 + PICKED] == PICKED
        far = lists[block * 16 + 8 + PICKED] == PICKED
        lines = slice(block * 8, block * 8 + 8)

        @pl.when(jnp.logical_not(jnp.logical_or(near, far)))
        def _(lines=lines):
            out[:, lines] = jnp.zeros((NX, 8, 16, 256), jnp.bfloat16)
            stat[:, lines] = jnp.full((NX, 8, 8, HEAD), FLOOR, jnp.float32)

        @pl.when(near)
        def _(block=block):
            unit(block, 0, False)

        @pl.when(jnp.logical_and(far, jnp.logical_not(near)))
        def _(block=block):
            unit(block, 1, False)

        @pl.when(jnp.logical_and(far, near))
        def _(block=block):
            unit(block, 1, True)

        @pl.when(jnp.logical_or(near, far))
        def _(block=block):
            for xd in range(NX):
                for r in range(2):
                    here = slice(block * 8 + r * 4, block * 8 + r * 4 + 4)
                    pieces = []
                    for half in range(2):
                        start = (2 * xd + half) * 2 + r
                        got = acc[pl.ds(start, 64, stride=16), :].astype(jnp.bfloat16)
                        out[xd, here, :, half * HEAD:(half + 1) * HEAD] = got.reshape(4, 16, HEAD)
                        pieces.append(tops[pl.ds(start, 64, stride=16), :].reshape(4, 16, HEAD))
                    low = jnp.where(lane < 32, pieces[0][:, :8], pieces[1][:, :8])
                    high = jnp.where(lane < 96, pieces[0][:, 8:], pieces[1][:, 8:])
                    stat[xd, here] = jnp.where(lane < 64, low, high)


def attend(lists, q, ko, vo, kp, vp):
    anywhere = pl.BlockSpec(memory_space=pl.ANY)
    inside = pl.BlockSpec(memory_space=VMEM)
    scalars = pl.BlockSpec(memory_space=pltpu.MemorySpace.SMEM)
    combos = BLOCKS * 2
    return pl.pallas_call(
        attend_kernel,
        out_shape=(
            jax.ShapeDtypeStruct((NX, NZ, 16, 256), jnp.bfloat16),
            jax.ShapeDtypeStruct((NX, NZ, 8, HEAD), jnp.float32),
        ),
        in_specs=[scalars, inside] + [anywhere] * 4,
        out_specs=(inside, inside),
        scratch_shapes=[
            pltpu.VMEM((combos, PICKED, 2 * PAGE, HEAD), jnp.bfloat16),
            pltpu.VMEM((combos, PICKED, 2 * PAGE, HEAD), jnp.bfloat16),
            pltpu.VMEM((PICKED, 2 * PAGE, HEAD), jnp.float32),
            pltpu.VMEM((PICKED * PAGE, HEAD), jnp.bfloat16),
            pltpu.VMEM((PICKED * PAGE, HEAD), jnp.bfloat16),
            pltpu.VMEM((PAGE * HEADS, HEAD), jnp.float32),
            pltpu.VMEM((PAGE * HEADS, HEAD), jnp.float32),
            DMA((combos, PICKED)),
            DMA((combos, PICKED)),
        ],
        name="attend",
    )(lists, q, ko, vo, kp, vp)


def blended(items):
    top = items[0][1]
    for _, level in items[1:]:
        top = jnp.maximum(top, level)
    shares = [jnp.exp(level - top) for _, level in items]
    total = shares[0]
    for share in shares[1:]:
        total = total + share
    scale = 1.0 / total
    lines = [[None, None], [None, None]]
    for (value, _), share in zip(items, shares):
        share = share * scale
        for band in range(2):
            for half in range(2):
                lane = band * 64 + half * 32
                term = value[band * 8:(band + 1) * 8, half * HEAD:(half + 1) * HEAD] * share[:, lane:lane + 1]
                before = lines[band][half]
                lines[band][half] = term if before is None else before + term
    value = jnp.concatenate([jnp.concatenate(line, axis=1) for line in lines], axis=0)
    return value, top + jnp.log(total)


def merge_kernel(
    part, stat, w, wp, result, got, got_stat, send, send_stat, land, land_stat, wcat,
    chunk, merged, terms, terms_in, sums, sums_in, lines,
    gs, gr, hs, hr, rs, rr, ts, tr, cs, ys, yr, ps, pr, zs, zr, xs, xr,
):
    x, z, c, y = place()
    other = {"c": 1 - c}
    xpeers = [{"x": around(x + j, NX)} for j in range(1, NX)]
    ypeers = [{"y": around(y + j, NY)} for j in range(1, NY)]
    zpeers = {hop: {"z": around(z + hop, NZ)} for hop in range(1, NZ)}
    greet([other] + xpeers + ypeers + [zpeers[hop] for hop in nearest(True)])
    started = []

    def go(copy):
        copy.start()
        started.append(copy)

    for j in range(1, NX):
        xd = around(x + j, NX)
        go(sent(stat.at[xd], got_stat.at[j - 1], hs.at[j - 1], hr.at[j - 1], xpeers[j - 1]))
    order = nearest(True) + [0]
    for number, hop in enumerate(order):
        slot = around(z + hop, NZ)
        for j in range(1, NX):
            xd = around(x + j, NX)
            go(sent(part.at[xd, slot], got.at[j - 1, slot], gs.at[j - 1, number], gr.at[j - 1, number], xpeers[j - 1]))
    wcat[c] = w[:, pl.ds(pl.multiple_of(c * 1024, 1024), 1024)]
    wcat[1 - c] = wp[...]
    for j in range(NX - 1):
        arrived(got_stat.at[j], hr.at[j])
    own = None
    for number, hop in enumerate(order):
        slot = around(z + hop, NZ)
        items = [(part[x, slot].astype(jnp.float32), stat[x, slot])]
        for j in range(NX - 1):
            arrived(got.at[j, slot], gr.at[j, number])
            items.append((got[j, slot].astype(jnp.float32), got_stat[j, slot]))
        value, level = blended(items)
        if hop == 0:
            own = value, level
        else:
            send[hop - 1] = value.astype(jnp.bfloat16)
            send_stat[hop - 1] = level
            go(sent(send_stat.at[hop - 1], land_stat.at[hop - 1], ts.at[hop - 1], tr.at[hop - 1], zpeers[hop]))
            go(sent(send.at[hop - 1], land.at[hop - 1], rs.at[hop - 1], rr.at[hop - 1], zpeers[hop]))
    items = [own]
    for hop in nearest():
        arrived(land_stat.at[hop - 1], tr.at[hop - 1])
        arrived(land.at[hop - 1], rr.at[hop - 1])
        items.append((land[hop - 1].astype(jnp.float32), land_stat[hop - 1]))
    chunk[...] = blended(items)[0].astype(jnp.bfloat16)
    for hop in nearest(True):
        go(sent(chunk, merged.at[x, z], zs.at[hop], zr.at[hop], zpeers[hop]))
    mine = pltpu.make_async_copy(chunk, merged.at[x, z], cs)
    mine.start()
    mine.wait()
    across(merged, z, 0, xs, xr, x, started)
    for number, hop in enumerate(nearest()):
        slot = around(z - hop, NZ)
        arrived(merged.at[x, slot], zr.at[hop])
        across(merged, slot, 1 + number, xs, xr, x, started)
    for number, hop in enumerate([0] + nearest()):
        crossed(merged, around(z - hop, NZ), number, xr, x)
    weight = wcat[...].reshape(128, 1024)
    total = None
    for xd in range(NX):
        term = lax.dot_general(
            merged[xd].reshape(256, 256),
            weight[:, xd * 256:(xd + 1) * 256],
            (((1,), (1,)), ((), ())),
            preferred_element_type=jnp.float32,
        )
        total = term if total is None else total + term
    total = total.reshape(2, 2, 2, 32, 128)
    for block in range(2):
        for near in range(2):
            terms[block * 2 + near] = total[block, :, near]
    for j in range(1, NY):
        go(sent(terms.at[around(y + j, NY)], terms_in.at[j - 1], ys.at[j - 1], yr.at[j - 1], ypeers[j - 1]))
    total = terms[y]
    for j in range(NY - 1):
        arrived(terms_in.at[j], yr.at[j])
        total = total + terms_in[j]
    sums[...] = total
    go(sent(sums, sums_in, ps, pr, other))
    arrived(sums_in, pr)
    total = sums[...] + sums_in[...]
    for r in range(2):
        lines[pl.ds(r, 32, stride=2), :] = total[r]
    total = lines[...]
    result[...] = jnp.where(c == 0, total[:, :64], total[:, 64:]).astype(jnp.bfloat16)
    for copy in started:
        copy.wait_send()


def merge(part, stat, w, wp):
    inside = pl.BlockSpec(memory_space=VMEM)
    piece = pltpu.VMEM((NZ - 1, 16, 256), jnp.bfloat16)
    level = pltpu.VMEM((NZ - 1, 8, HEAD), jnp.float32)
    return pl.pallas_call(
        merge_kernel,
        out_shape=jax.ShapeDtypeStruct((64, 64), jnp.bfloat16),
        in_specs=[inside] * 4,
        out_specs=inside,
        scratch_shapes=[
            pltpu.VMEM((NX - 1, NZ, 16, 256), jnp.bfloat16),
            pltpu.VMEM((NX - 1, NZ, 8, HEAD), jnp.float32),
            piece, level, piece, level,
            pltpu.VMEM((2, 64, 1024), jnp.bfloat16),
            pltpu.VMEM((16, 256), jnp.bfloat16),
            pltpu.VMEM((NX, NZ, 16, 256), jnp.bfloat16),
            pltpu.VMEM((NY, 2, 32, 128), jnp.float32),
            pltpu.VMEM((NY - 1, 2, 32, 128), jnp.float32),
            pltpu.VMEM((2, 32, 128), jnp.float32),
            pltpu.VMEM((2, 32, 128), jnp.float32),
            pltpu.VMEM((64, 128), jnp.float32),
            DMA((NX - 1, NZ)), DMA((NX - 1, NZ)), DMA((NX - 1,)), DMA((NX - 1,)),
            DMA((NZ - 1,)), DMA((NZ - 1,)), DMA((NZ - 1,)), DMA((NZ - 1,)),
            DMA, DMA((NY - 1,)), DMA((NY - 1,)), DMA, DMA, DMA((NZ,)), DMA((NZ,)),
        ] + X_SEMS,
        compiler_params=pltpu.CompilerParams(collective_id=1, has_side_effects=True),
        name="merge",
    )(part, stat, w, wp)


def per_device(queries, cached_keys, cached_values, out_weight, select, page_table, block_page):
    q = queries.reshape(2, 2 * HEADS, HEAD).transpose(1, 0, 2).reshape(2, 16, HEAD)
    k = cached_keys.reshape(PAGES_DEV, 2 * PAGE, HEAD)
    v = cached_values.reshape(PAGES_DEV, 2 * PAGE, HEAD)
    w = out_weight.T
    lists, qall, kp, vp, wp = collect(select, page_table, block_page, q, k, v, w)
    part, stat = attend(lists, qall, k, v, kp, vp)
    return merge(part, stat, w, wp)


def solution(mesh):
    torus = Mesh(mesh.devices.reshape(NX, NZ, 2, NY), ("x", "z", "c", "y"))
    return jax.shard_map(
        per_device,
        mesh=torus,
        in_specs=(
            P(PAGES, "y"),
            P(PAGES, None, "y", None),
            P(PAGES, None, "y", None),
            P("y", PAGES),
            P(),
            P(),
            P(),
        ),
        out_specs=P("y", PAGES),
        check_vma=False,
    )
```

time: 120 us -> 91.4 us (0.76)
  Pallas kernels: 117 us -> 90.2 us
  local copies, waits for them, and re-layouts: 2.62 us -> 1.32 us
    pallas_call x1, Pallas kernels: 76.6 us -> 52.6 us  [merge(): pl.pallas_call(merge_kernel, out_shape=jax.ShapeDtypeStruct((64, 64), jnp...]
    pallas_call x1, Pallas kernels: 36.5 us -> 34.8 us  [collect(): pl.pallas_call(collect_kernel, out_shape=(jax.ShapeDtypeStruct((BLOCKS *...]
    pallas_call x1, Pallas kernels: 4.06 us -> 2.75 us  [attend(): pl.pallas_call(attend_kernel, out_shape=(jax.ShapeDtypeStruct((NX, NZ, 16...]
    reshape x1 -> x0, local copies, waits for them, and re-layouts: 1.3 us -> none  [per_device(): queries.reshape(2, 2, HEADS, HEAD).transpose(1, 0, 2, 3)]
where the time goes in v1:
time: 91.4 us; the launch traced here: 91.5 us
  Pallas kernels  90.2 us (99%)
  local copies, waits for them, and re-layouts  1.32 us (1%)
    pallas_call x1, Pallas kernels, merge(): pl.pallas_call(merge_kernel, out_shape=jax.ShapeDtypeStruct((64, 64), jnp...  52.6 us
    pallas_call x1, Pallas kernels, collect(): pl.pallas_call(collect_kernel, out_shape=(jax.ShapeDtypeStruct((BLOCKS *...  34.8 us
    pallas_call x1, Pallas kernels, attend(): pl.pallas_call(attend_kernel, out_shape=(jax.ShapeDtypeStruct((NX, NZ, 16...  2.75 us

profile of v1, /device:TPU:1, one launch (start us, length us, event | category | flops | bytes accessed | tf_op | source)
XLA Modules:
  0.0 91.5 jit_solution(5875215873566960228)
XLA Ops:
  0.0 34.8 %collect.1 = (s32[32]{0:T(128)}, bf16[4,16,2,16,128]{4,3,2,1,0:T(8,128)(2,1)}, bf16[16,256,128]{2,1,0:T(8,128)(2,1)}, bf16[16,256,128]{2,1,0:T(8,128)(2,1)}, bf16[64,1024]{1,0:T(8,128)(2,1)}) custom-call(s32[2,24]{1,0:T(2,128)} %select.1, s32[2048]{0:T(1024)} %table.1, s32[2]{0:T(128)} %block_page.1, bf16[2,16,128]{2,1,0:T(8,128)(2,1)} %bitcast.14, ...), custom_call_target="tpu_custom_call" | custom-call | tf_op jit(solution)/shard_map/collect/pallas_call | solution.py:156
  34.9 2.8 %attend.1 = (bf16[4,16,16,256]{3,2,1,0:T(8,128)(2,1)}, f32[4,16,8,128]{3,2,1,0:T(8,128)}) custom-call(s32[32]{0:T(128)} %get-tuple-element.12.lists, bf16[4,16,2,16,128]{4,3,2,1,0:T(8,128)(2,1)} %get-tuple-element.13.q, bf16[16,256,128]{2,1,0:T(8,128)(2,1)} %bitcast.9, bf16[16,256,128]{2,1,0:T(8,128)(2,1)} %bitcast.11, ...), custom_call_target="tpu_custom_call" | custom-call | tf_op jit(solution)/shard_map/attend/pallas_call | solution.py:271
  37.6 52.6 %merge.1 = bf16[64,64]{1,0:T(8,128)(2,1)} custom-call(bf16[4,16,16,256]{3,2,1,0:T(8,128)(2,1)} %get-tuple-element.16.part, f32[4,16,8,128]{3,2,1,0:T(8,128)} %get-tuple-element.17.stat, bf16[64,2048]{1,0:T(8,128)(2,1)} %bitcast.13, bf16[64,1024]{1,0:T(8,128)(2,1)} %get-tuple-element.18.wp), custom_call_target="tpu_custom_call" | custom-call | tf_op jit(solution)/shard_map/merge/pallas_call | solution.py:415
  90.2 1.3 %copy.10 = bf16[64,64]{1,0:T(8,128)(2,1)} copy(bf16[64,64]{1,0:T(8,128)(2,1)} %merge.1) | data formatting | bytes 16384
